TPU v7x, 32 devices: a whole 2x2x4 slice. The times are simulated.
32 devices in a mesh: replica: 4 (over y, core), table: 8 (over z, x).
Axes of the slice: x: 2, y: 2, z: 4, core: 2. Of those that a mesh axis runs over, the one named last changes fastest.
Arguments:
- cache: float32 [768, 16384], P('table', 'replica'), may hold values from -6 to 6
- accum: float32 [768, 16384], P('table', 'replica'), may hold values from 0.5 to 8
- row_ids: int32 [4, 8, 128], P('replica'), may hold values from 0 to 4095
- lengths: int32 [4, 8], P('replica'), may hold values from 1 to 128, 614 in all within a row
- seq_slot: int32 [4, 8], P('replica'), may hold values from 0 to 7, each once within a row
- block_mask: int32 [4, 8, 2, 2], P('replica'), may hold values 0 or 1
- cotangent: bfloat16 [4, 1024, 768], P('replica', 'table'), may hold values from -6 to 6
- w_uqkv: bfloat16 [768, 3072], P('replica'), may hold values from -0.21875 to 0.21875
- w_out: bfloat16 [768, 768], P('replica'), may hold values from -0.21875 to 0.21875
- w2_accum: float32 [768, 768], P('replica', 'table'), may hold values from 81.92 to 8192
Outputs:
- cache_new: float32 [768, 16384], P('table', 'replica')
- accum_new: float32 [768, 16384], P('table', 'replica')
- w2_step: float32 [768, 768], P('replica', 'table')
Inputs may be any that keep to these rules, and one draw needn't show every extreme that they name: `lengths`: in every replica group some sequence has length 128. `seq_slot`: each row names every slot once.
All inputs are finite; a program needn't handle non-finite values. No bound on the sum of `block_mask` on one device may be relied on, other than what follows from the above.
Results may differ from a plain program's by a relative error of at most 0.012.
Values may be sent and summed in bfloat16 or wider, within the bound.
A program may use at most 64 MiB of HBM per device.

v0:
```python
from functools import partial

import jax
import jax.numpy as jnp
from jax import lax
from jax.sharding import PartitionSpec as P

D = 768
HEADS = 12
HEAD_DIM = 64
SEQ_DEV = 1
SEQ_LEN = 128
CAP = 128


EPS_NORM = 1e-05
EPS_ATTN = 1e-06
STEP_SIZE = 0.5


def normalize(row_data):
    centred = row_data - jnp.mean(row_data, axis=-1, keepdims=True)
    variance = jnp.mean(centred * centred, axis=-1, keepdims=True)
    return centred / jnp.sqrt(variance + EPS_NORM)


def pattern_mask(lengths_at, blocks_at, seq_len):
    block_count = blocks_at.shape[-1]
    block_width = seq_len // block_count
    places = jnp.arange(seq_len, dtype=jnp.int32)
    block_of = places // block_width
    same_block = block_of[:, None] == block_of[None, :]
    chosen = jnp.repeat(jnp.repeat(blocks_at, block_width, axis=1), block_width, axis=2) > 0
    chosen = chosen | same_block[None]
    causal = places[None, :] <= places[:, None]
    inside = places[None, :] < lengths_at[:, None]
    allowed = chosen & causal[None] & inside[:, :, None] & inside[:, None, :]
    return (allowed.astype(jnp.float32), inside)


def attention_branch(hidden_pre, allowed):
    slot_count = allowed.shape[0]
    seq_len = allowed.shape[1]
    projected = jax.nn.silu(hidden_pre).astype(jnp.bfloat16)
    gate_u = projected[:, :D]
    queries = projected[:, D : 2 * D].reshape(slot_count, seq_len, HEADS, HEAD_DIM)
    key_rows = projected[:, 2 * D : 3 * D].reshape(slot_count, seq_len, HEADS, HEAD_DIM)
    value_rows = projected[:, 3 * D :].reshape(slot_count, seq_len, HEADS, HEAD_DIM)
    scores = jnp.einsum(
        "sihd,sjhd->shij", queries, key_rows, preferred_element_type=jnp.float32
    ) * HEAD_DIM ** (-0.5)
    weights = (jax.nn.silu(scores) * allowed[:, None]).astype(jnp.bfloat16)
    attended = jnp.einsum(
        "shij,sjhd->sihd", weights, value_rows, preferred_element_type=jnp.float32
    )
    attended = attended.reshape(slot_count * seq_len, D)
    centred_att = attended - jnp.mean(attended, axis=-1, keepdims=True)
    inverse_dev = 1.0 / jnp.sqrt(
        jnp.mean(centred_att * centred_att, axis=-1, keepdims=True) + EPS_ATTN
    )
    return centred_att * inverse_dev * gate_u.astype(jnp.float32)


def body(cache, accum, row_ids, lengths, seq_slot, block_mask, cotangent, w_uqkv, w_out, w2_accum):
    tables = lax.axis_size("table")
    table_index = lax.axis_index("table")
    columns = cache.shape[0]
    seq_count = seq_slot.shape[1]
    sequence_ids = jnp.arange(seq_count, dtype=jnp.int32)
    matches = (seq_slot[0][:, None] == sequence_ids[None, :]).astype(jnp.int32)
    seq_at = jnp.sum(sequence_ids[:, None] * matches, axis=0)
    lengths_at = jnp.sum(lengths[0][:, None] * matches, axis=0)
    slot_ids = row_ids[0][seq_at].reshape(-1)
    own_first = table_index * SEQ_DEV
    own_lengths = lax.dynamic_slice_in_dim(lengths_at, own_first, SEQ_DEV, 0)
    own_blocks = lax.dynamic_slice_in_dim(block_mask[0][seq_at], own_first, SEQ_DEV, 0)
    allowed, inside = pattern_mask(own_lengths, own_blocks, SEQ_LEN)
    picked = jnp.take(cache, slot_ids, axis=1).astype(jnp.bfloat16).reshape(columns, tables, CAP)
    arrived = lax.all_to_all(picked, "table", split_axis=1, concat_axis=0, tiled=True)
    embedded = arrived.reshape(D, CAP).T
    row_float = embedded.astype(jnp.float32)
    normed = normalize(row_float).astype(jnp.bfloat16)
    full_uqkv = lax.all_gather(w_uqkv, "replica", axis=0, tiled=True)
    hidden_pre = jnp.dot(normed, full_uqkv, preferred_element_type=jnp.float32)
    live_cot = cotangent[0] * inside.reshape(-1)[:, None].astype(jnp.bfloat16)
    d_gated = lax.dot_general(
        live_cot,
        lax.all_gather(w_out, "replica", axis=0, tiled=True),
        (((1,), (1,)), ((), ())),
        preferred_element_type=jnp.float32,
    )
    gated_raw, branch_vjp = jax.vjp(partial(attention_branch, allowed=allowed), hidden_pre)
    gated = gated_raw.astype(jnp.bfloat16)
    d_hidden = branch_vjp(d_gated)[0].astype(jnp.bfloat16)
    d_normed = lax.dot_general(
        d_hidden, full_uqkv, (((1,), (1,)), ((), ())), preferred_element_type=jnp.float32
    )
    _, norm_vjp = jax.vjp(normalize, row_float)
    row_grad = live_cot.astype(jnp.float32) + norm_vjp(d_normed)[0]
    sending = row_grad.T.reshape(tables, columns, CAP)
    returned = lax.all_to_all(sending, "table", split_axis=0, concat_axis=2, tiled=True).reshape(
        columns, tables * CAP
    )
    grad_cols = jnp.zeros_like(cache).at[:, slot_ids].add(returned)
    accum_next = accum + grad_cols * grad_cols
    cache_next = cache - STEP_SIZE * grad_cols / jnp.sqrt(accum_next)
    full_grad = lax.dot_general(
        gated, live_cot, (((0,), (0,)), ((), ())), preferred_element_type=jnp.float32
    )
    by_columns = lax.psum_scatter(full_grad, "table", scatter_dimension=1, tiled=True)
    summed = lax.psum_scatter(by_columns, "replica", scatter_dimension=0, tiled=True)
    w2_step = summed / jnp.sqrt(w2_accum + summed * summed)
    return (cache_next, accum_next, w2_step)


def solution(mesh):
    return jax.shard_map(
        body,
        mesh=mesh,
        in_specs=(
            P("table", "replica"),
            P("table", "replica"),
            P("replica", None, None),
            P("replica", None),
            P("replica", None),
            P("replica", None, None, None),
            P("replica", "table", None),
            P("replica", None),
            P("replica", None),
            P("replica", "table"),
        ),
        out_specs=(P("table", "replica"), P("table", "replica"), P("replica", "table")),
        check_vma=False,
    )
```

profile of v0, /device:TPU:1, one launch (start us, length us, event | category | flops | bytes accessed | tf_op | source)
XLA Modules:
  0.0 179.3 jit_solution(12258738646778073409)
XLA Ops:
  7.2 0.7 all-gather.5.cloned.1.call-update
  7.9 1.8 %copy.119 = f32[96,4096]{0,1:T(8,128)S(1)} copy(f32[96,4096]{1,0:T(8,128)} %param.10) | data formatting | bytes 3145728 | tf_op args[0]
  9.9 0.6 gather_fusion
  10.5 2.9 %gather_fusion.1 = bf16[1024,96]{1,0:T(8,128)(2,1)S(1)} fusion(f32[96,4096]{0,1:T(8,128)S(1)} %copy.119, s32[1024]{0:T(1024)S(1)} %broadcast_clamp_fusion), kind=kCustom, calls=%fused_computation.1 | custom fusion | bytes 397312 | tf_op jit(solution)/shard_map/jit(_take)/gather | solution.py:78
  13.4 0.2 copy.102
  13.6 0.7 select_convert_fusion
  14.3 6.3 %all-to-all-start = ((bf16[96,8,128]{2,0,1:T(8,128)(2,1)}), bf16[96,8,128]{2,0,1:T(8,128)(2,1)S(1)}, u32[]{:S(2)}, u32[]{:S(2)}) async-start(bf16[96,8,128]{2,0,1:T(8,128)(2,1)} %select_convert_fusion), calls=%async_computation | async-start | bytes 393216 | tf_op jit(solution)/shard_map/all_to_all | solution.py:79
  20.7 0.7 all-gather.3.cloned.1.call-update
  21.5 0.1 copy.107
  21.6 0.6 gather_fusion.2
  22.2 0.6 dynamic_slice.6
  22.7 0.1 copy.108
  23.0 0.7 iota_compare_fusion.2
  23.7 0.1 fusion.41
  23.9 0.7 fusion.48
  24.5 2.8 %all-to-all-done = bf16[96,8,128]{2,0,1:T(8,128)(2,1)S(1)} async-done(((bf16[96,8,128]{2,0,1:T(8,128)(2,1)}), bf16[96,8,128]{2,0,1:T(8,128)(2,1)S(1)}, u32[]{:S(2)}, u32[]{:S(2)}) %all-to-all-start) | async-done | bytes 196640 | tf_op jit(solution)/shard_map/all_to_all | solution.py:79
  27.3 0.2 copy.103
  27.5 0.1 convert_reduce_fusion
  27.6 0.2 fusion.23
  27.8 0.5 multiply_divide_fusion
  28.4 21.1 %all-gather.5.cloned.1.call-done = bf16[768,3072]{1,0:T(8,128)(2,1)} async-done(((bf16[192,3072]{1,0:T(8,128)(2,1)}), bf16[768,3072]{1,0:T(8,128)(2,1)}) %all-gather.5.cloned.1.call-update) | async-done | bytes 4718608 | tf_op jit(solution)/shard_map/all_gather | solution.py:83
  49.5 4.4 %multiply_convert_fusion = (bf16[128,3072]{1,0:T(8,128)(2,1)S(1)}, f32[128,3072]{1,0:T(8,128)}) fusion(bf16[768,3072]{1,0:T(8,128)(2,1)} %all-gather.5.cloned.1.call-done, f32[768,128]{0,1:T(8,128)S(1)} %copy.103, f32[128]{0:T(128)S(1)} %get-tuple-element.31, f32[128]{0:T(128)S(1)} %broadcast_multiply_fusion.1), kind=kOutput, calls=%fused_computation.12 | convolution fusion | flops 606240768 | bytes 7472128 | tf_op jit(solution)/shard_map/dot_general | solution.py:84
  53.9 0.9 copy-done.2
  54.8 0.8 copy.104
  55.6 0.2 copy.105
  55.8 0.2 copy.106
  56.0 1.3 multiply_convert_fusion.1
  57.3 1.0 fusion.52
  58.3 0.2 copy.110
  58.5 0.7 broadcast_multiply_fusion
  59.1 0.7 fusion.22
  59.8 8.7 %all-gather.3.cloned.1.call-done = bf16[768,768]{1,0:T(8,128)(2,1)} async-done(((bf16[192,768]{1,0:T(8,128)(2,1)}), bf16[768,768]{1,0:T(8,128)(2,1)}) %all-gather.3.cloned.1.call-update) | async-done | bytes 1179664 | tf_op jit(solution)/shard_map/all_gather | solution.py:88
  68.5 1.9 %multiply_reduce_fusion = (f32[128]{0:T(128)S(1)}, f32[128,768]{1,0:T(8,128)S(1)}) fusion(f32[128,768]{1,0:T(8,128)S(1)} %copy.110, f32[128]{0:T(128)S(1)} %broadcast_multiply_fusion, bf16[128,3072]{1,0:T(8,128)(2,1)} %copy-done.2, bf16[768,768]{1,0:T(8,128)(2,1)} %all-gather.3.cloned.1.call-done, bf16[1,128,768]{2,1,0:T(8,128)(2,1)S(1)} %copy-done.3, ...), kind=kOutput, calls=%fused_computation.56 | convolution fusion | flops 151584640 | bytes 2360576 | tf_op jit(solution)/shard_map/dot_general | solution.py:86
  70.5 0.5 fusion.43
  71.0 0.6 copy-done.12
  71.6 3.0 %fusion.28 = f32[768,768]{0,1:T(8,128)} fusion(f32[128,768]{1,0:T(8,128)S(1)} %copy.110, f32[128]{0:T(128)S(1)} %broadcast_multiply_fusion, f32[128]{0:T(128)S(1)} %get-tuple-element.33, bf16[1,128,768]{2,1,0:T(8,128)(2,1)S(1)} %copy-done.3, bf16[128,3072]{1,0:T(8,128)(2,1)} %copy-done.2, bf16[128]{0:T(256)(128)(2,1)S(1)} %fusion.48), kind=kOutput, calls=%fused_computation.59 | convolution fusion | flops 151584768 | bytes 3147008 | tf_op jit(solution)/shard_map/dot_general | solution.py:107
  74.5 1.8 %fusion.50 = (f32[128]{0:T(128)S(1)}, f32[128,768]{1,0:T(8,128)S(1)}, bf16[128,768]{1,0:T(8,128)(2,1)}) fusion(f32[128]{0:T(128)} %get-tuple-element.32, f32[128,768]{1,0:T(8,128)S(1)} %copy.110, f32[128]{0:T(128)S(1)} %broadcast_multiply_fusion, f32[128]{0:T(128)} %copy-done.12, f32[128,768]{1,0:T(8,128)S(1)} %get-tuple-element.41, ...), kind=kLoop, calls=%fused_computation.111 | loop fusion | flops 1081216 | bytes 1574912 | tf_op jit(solution)/shard_map/transpose(jvp())/reduce_sum | solution.py:57
  76.5 0.2 copy.111
  76.6 0.7 copy-done.10
  77.3 1.8 %fusion.11 = bf16[12,128,128]{2,1,0:T(8,128)(2,1)S(1)} fusion(f32[12,128,128]{2,1,0:T(8,128)} %get-tuple-element.37, bf16[12,64,128]{2,1,0:T(8,128)(2,1)S(1)} %bitcast.128, bf16[128,12,64]{0,2,1:T(8,128)(2,1)} %bitcast.122, f32[128,128]{1,0:T(8,128)S(1)} %copy.109), kind=kOutput, calls=%fused_computation.27 | convolution fusion | flops 27721728 | bytes 1638400 | tf_op jit(solution)/shard_map/transpose(jvp(shij,sjhd->sihd))/dot_general | solution.py:53
  79.1 1.1 fusion.54
  80.2 1.8 copy.114
  82.0 1.8 %fusion.55 = bf16[12,128,64]{1,2,0:T(8,128)(2,1)} fusion(bf16[12,128,128]{2,1,0:T(8,128)(2,1)S(1)} %fusion.11, bf16[128,12,64]{0,2,1:T(8,128)(2,1)} %bitcast.125), kind=kOutput, calls=%fused_computation.116 | convolution fusion | flops 25165824 | bytes 786432 | tf_op jit(solution)/shard_map/transpose(jvp(sihd,sjhd->shij))/dot_general | solution.py:49
  83.8 1.7 copy.113
  85.5 1.2 fusion.53
  86.7 0.1 copy.112
  86.9 5.0 %fusion.25 = (f32[128]{0:T(128)S(1)}, f32[128,768]{1,0:T(8,128)S(1)}) fusion(f32[768,128]{0,1:T(8,128)S(1)} %copy.103, f32[128]{0:T(128)S(1)} %copy-done.23, f32[128]{0:T(128)S(1)} %copy-done.14, bf16[768,3072]{1,0:T(8,128)(2,1)} %all-gather.5.cloned.1.call-done, f32[128,3072]{1,0:T(8,128)} %get-tuple-element.35, bf16[128,768]{1,0:T(8,128)(2,1)} %get-tuple-element.26, ...), kind=kOutput, calls=%fused_computation.53 | convolution fusion | flops 611450752 | bytes 7865856 | tf_op jit(solution)/shard_map/dot_general | solution.py:95
  92.0 0.2 fusion.49
  92.2 0.1 add_bitcast_fusion
  92.3 0.9 copy.115
  93.3 5.2 %all-to-all-start.1 = ((f32[8,96,128]{2,1,0:T(8,128)}), f32[8,96,128]{2,1,0:T(8,128)S(1)}, u32[]{:S(2)}, u32[]{:S(2)}) async-start(f32[8,96,128]{2,1,0:T(8,128)} %bitcast.40), calls=%async_computation.1 | async-start | bytes 786432 | tf_op jit(solution)/shard_map/all_to_all | solution.py:101
  98.6 2.8 %copy.118 = f32[96,4096]{0,1:T(8,128)} copy(f32[96,4096]{1,0:T(8,128)} %param.11) | data formatting | bytes 3145728 | tf_op args[1]
  101.5 13.0 %all-to-all-done.1 = f32[8,96,128]{2,1,0:T(8,128)S(1)} async-done(((f32[8,96,128]{2,1,0:T(8,128)}), f32[8,96,128]{2,1,0:T(8,128)S(1)}, u32[]{:S(2)}, u32[]{:S(2)}) %all-to-all-start.1) | async-done | bytes 393248 | tf_op jit(solution)/shard_map/all_to_all | solution.py:101
  114.5 0.2 copy.116
  114.8 0.2 copy.117
  115.0 7.4 %scatter_custom_fusion = f32[96,4096]{0,1:T(8,128)} fusion(s32[1024]{0:T(1024)S(1)} %bitcast.135, f32[1024,96]{1,0:T(8,128)S(1)} %copy.117, f32[]{:T(128)} %constant.61.clone.1), kind=kCustom, calls=%fused_computation.22 | custom fusion | flops 98304 | bytes 1572868 | tf_op jit(solution)/shard_map/scatter-add | solution.py:104
  122.4 25.0 %reduce-scatter.5.cloned.1.call-done = f32[768,96]{0,1:T(8,128)} async-done(((f32[768,768]{0,1:T(8,128)}), f32[768,96]{0,1:T(8,128)}) %reduce-scatter.5.cloned.1.call-update) | async-done | bytes 294928 | tf_op jit(solution)/shard_map/reduce_scatter | solution.py:110
  147.4 1.9 %copy.124 = f32[768,96]{1,0:T(8,128)} copy(f32[768,96]{0,1:T(8,128)} %reduce-scatter.5.cloned.1.call-done) | data formatting | bytes 589824
  149.3 4.6 %multiply_subtract_fusion = (f32[96,4096]{0,1:T(8,128)}, f32[96,4096]{0,1:T(8,128)}) fusion(f32[96,4096]{0,1:T(8,128)S(1)} %copy.119, f32[96,4096]{0,1:T(8,128)} %scatter_custom_fusion, f32[96,4096]{0,1:T(8,128)} %copy.118), kind=kLoop, calls=%fused_computation.5 | loop fusion | flops 1966080 | bytes 7864320 | tf_op jit(solution)/shard_map/sub | solution.py:106
  154.0 2.9 %copy.121 = f32[96,4096]{1,0:T(8,128)} copy(f32[96,4096]{0,1:T(8,128)} %get-tuple-element.20) | data formatting | bytes 3145728
  156.9 1.7 copy.122
  158.6 12.4 %reduce-scatter.7.cloned.1.call-done = f32[192,96]{1,0:T(8,128)} async-done(((f32[768,96]{1,0:T(8,128)}), f32[192,96]{1,0:T(8,128)}) %reduce-scatter.7.cloned.1.call-update) | async-done | bytes 73744
  171.0 1.0 copy.125
  172.0 0.7 copy.123
  (72 shorter events, 1.0 us)
Async XLA Ops:
  7.2 2.7 %copy-start = (s32[1,8,128]{2,1,0:T(8,128)S(1)}, s32[1,8,128]{2,1,0:T(8,128)}, u32[]{:S(2)}) copy-start(s32[1,8,128]{2,1,0:T(8,128)} %param.12) | copy-start | bytes 12292
  7.2 42.3 %all-gather.5.cloned.1.call-start = ((), (), s32[]{:S(2)}) async-start(), calls=%async_computation.5 | async-start | bytes 5898240 | tf_op jit(solution)/shard_map/all_gather | solution.py:83
  7.9 1.9 %copy-start.21 = (s32[1,8]{1,0:T(1,128)S(1)}, s32[1,8]{1,0:T(1,128)}, u32[]{:S(2)}) copy-start(s32[1,8]{1,0:T(1,128)} %param.13) | copy-start | bytes 100
  7.9 1.9 %copy-start.22 = (s32[1,8]{1,0:T(1,128)S(1)}, s32[1,8]{1,0:T(1,128)}, u32[]{:S(2)}) copy-start(s32[1,8]{1,0:T(1,128)} %param.14) | copy-start | bytes 100
  10.5 11.0 %copy-start.16 = (s32[1,8,2,2]{1,3,2,0:T(2,128)S(1)}, s32[1,8,2,2]{1,3,2,0:T(2,128)}, u32[]{:S(2)}) copy-start(s32[1,8,2,2]{1,3,2,0:T(2,128)} %param.15) | copy-start | bytes 388
  14.3 13.0 %all-to-all-start = ((bf16[96,8,128]{2,0,1:T(8,128)(2,1)}), bf16[96,8,128]{2,0,1:T(8,128)(2,1)S(1)}, u32[]{:S(2)}, u32[]{:S(2)}) async-start(bf16[96,8,128]{2,0,1:T(8,128)(2,1)} %select_convert_fusion), calls=%async_computation | async-start | bytes 393216 | tf_op jit(solution)/shard_map/all_to_all | solution.py:79
  20.7 47.8 %all-gather.3.cloned.1.call-start = ((), (), s32[]{:S(2)}) async-start(), calls=%async_computation.4 | async-start | bytes 1474560 | tf_op jit(solution)/shard_map/all_gather | solution.py:88
  21.4 126.0 %reduce-scatter.5.cloned.1.call-start = ((), (), s32[]{:S(2)}) async-start(), calls=%async_computation.6 | async-start | bytes 2654208 | tf_op jit(solution)/shard_map/reduce_scatter | solution.py:110
  27.6 26.2 %copy-start.13 = (f32[128]{0:T(128)}, f32[128]{0:T(128)S(1)}, u32[]{:S(2)}) copy-start(f32[128]{0:T(128)S(1)} %broadcast_multiply_fusion.1) | copy-start | bytes 1540
  27.8 26.0 %copy-start.19 = (f32[128]{0:T(128)}, f32[128]{0:T(128)S(1)}, u32[]{:S(2)}) copy-start(f32[128]{0:T(128)S(1)} %fusion.23) | copy-start | bytes 1540
  28.4 25.5 %copy-start.17 = (f32[128]{0:T(128)}, f32[128]{0:T(128)S(1)}, u32[]{:S(2)}) copy-start(f32[128]{0:T(128)S(1)} %get-tuple-element.31) | copy-start | bytes 1540
  53.9 0.9 copy-start.2
  55.8 1.5 copy-start.7
  55.9 1.4 copy-start.8
  56.0 1.4 copy-start.6
  57.3 1.0 copy-start.4
  57.3 11.2 %copy-start.3 = (bf16[1,128,768]{2,1,0:T(8,128)(2,1)S(1)}, bf16[1,128,768]{2,1,0:T(8,128)(2,1)}, u32[]{:S(2)}) copy-start(bf16[1,128,768]{2,1,0:T(8,128)(2,1)} %param.16) | copy-start | bytes 589828
  68.5 1.9 %copy-start.15 = (f32[128]{0:T(128)S(1)}, f32[128]{0:T(128)}, u32[]{:S(2)}) copy-start(f32[128]{0:T(128)} %fusion.22) | copy-start | bytes 1540
  71.0 0.6 copy-start.12
  76.6 0.7 copy-start.10
  77.3 1.8 %copy-start.9 = (bf16[128,768]{0,1:T(8,128)(2,1)S(1)}, bf16[128,768]{0,1:T(8,128)(2,1)}, u32[]{:S(2)}) copy-start(bf16[128,768]{0,1:T(8,128)(2,1)} %copy-done.8) | copy-start | bytes 589828
  79.1 6.4 %copy-start.5 = (bf16[12,128,128]{2,1,0:T(8,128)(2,1)S(1)}, bf16[12,128,128]{2,1,0:T(8,128)(2,1)}, u32[]{:S(2)}) copy-start(bf16[12,128,128]{2,1,0:T(8,128)(2,1)} %copy-done.4) | copy-start | bytes 1179652
  80.2 6.7 %copy-start.14 = (f32[128]{0:T(128)S(1)}, f32[128]{0:T(128)}, u32[]{:S(2)}) copy-start(f32[128]{0:T(128)} %copy-done.13) | copy-start | bytes 1540
  80.2 6.7 %copy-start.23 = (f32[128]{0:T(128)S(1)}, f32[128]{0:T(128)}, u32[]{:S(2)}) copy-start(f32[128]{0:T(128)} %get-tuple-element.30) | copy-start | bytes 1540
  86.9 5.0 %copy-start.20 = (f32[128]{0:T(128)S(1)}, f32[128]{0:T(128)}, u32[]{:S(2)}) copy-start(f32[128]{0:T(128)} %copy-done.19) | copy-start | bytes 1540
  86.9 5.1 %copy-start.18 = (f32[128]{0:T(128)S(1)}, f32[128]{0:T(128)}, u32[]{:S(2)}) copy-start(f32[128]{0:T(128)} %copy-done.17) | copy-start | bytes 1540
  93.3 21.3 %all-to-all-start.1 = ((f32[8,96,128]{2,1,0:T(8,128)}), f32[8,96,128]{2,1,0:T(8,128)S(1)}, u32[]{:S(2)}, u32[]{:S(2)}) async-start(f32[8,96,128]{2,1,0:T(8,128)} %bitcast.40), calls=%async_computation.1 | async-start | bytes 786432 | tf_op jit(solution)/shard_map/all_to_all | solution.py:101
  98.5 2.9 %copy-start.11 = (f32[192,96]{1,0:T(8,128)S(1)}, f32[192,96]{1,0:T(8,128)}, u32[]{:S(2)}) copy-start(f32[192,96]{1,0:T(8,128)} %param.19) | copy-start | bytes 221188
  98.5 72.5 %reduce-scatter.7.cloned.1.call-start = ((), (), s32[]{:S(2)}) async-start(), calls=%async_computation.7 | async-start | bytes 491520
  154.0 2.9 %copy-start.1 = (f32[96,4096]{0,1:T(8,128)S(1)}, f32[96,4096]{0,1:T(8,128)}, u32[]{:S(2)}) copy-start(f32[96,4096]{0,1:T(8,128)} %get-tuple-element.21) | copy-start | bytes 4718596
Sparse Core Ops, SparseCore 0:
  9.5 39.8 all-gather.4
  51.0 17.4 all-gather.2
  74.7 72.6 reduce-scatter.4
  149.8 21.1 reduce-scatter.6
where the time goes:
time: 181 us; the launch traced here: 179 us
  waiting for transfers between devices  84.4 us (47%)
  local copies, waits for them, and re-layouts  27.2 us (15%)
  matrix products  22.4 us (12%)
  other arithmetic  19.4 us (11%)
  between operations  14.2 us (8%)
  starting transfers between devices  11.7 us (6%)
    reduce_scatter x1, waiting for transfers between devices, body(): lax.psum_scatter(full_grad, 'table', scatter_dimension=1, tiled=True)  25 us
    all_gather x1, waiting for transfers between devices, body(): full_uqkv = lax.all_gather(w_uqkv, 'replica', axis=0, tiled=True)  21.1 us
    unnamed x57, local copies, waits for them, and re-layouts  15.3 us
    unnamed x5, waiting for transfers between devices  13.8 us
    all_to_all x1, waiting for transfers between devices, body(): lax.all_to_all(sending, 'table', split_axis=0, concat_axis=2, tiled=True)  13 us
    all_gather x1, waiting for transfers between devices, body(): lax.all_gather(w_out, 'replica', axis=0, tiled=True)  8.67 us
    scatter-add x1, other arithmetic, body(): grad_cols = jnp.zeros_like(cache).at[:, slot_ids].add(returned)  7.41 us
    all_to_all x1, starting transfers between devices, body(): lax.all_to_all(picked, 'table', split_axis=1, concat_axis=0, tiled=True)  6.34 us
  transfers between devices with their start and end apart: 6, of which 6 were waited for; matrix products, arithmetic and copies ran while one was open for 32% of the time, Pallas kernels for 0%

commit v1 on v0

v1 whole, which is shorter than its diff:
```python
import functools

import jax
import jax.numpy as jnp
from jax import lax
from jax.experimental import pallas as pl
from jax.experimental.pallas import tpu as pltpu
from jax.sharding import PartitionSpec as P

D = 768
HEADS = 12
HEAD_DIM = 64
EPS_NORM = 1e-05
EPS_ATTN = 1e-06
STEP_SIZE = 0.5
PAIR = 2 * HEAD_DIM
CHUNK = 512

F32 = jnp.float32
BF16 = jnp.bfloat16

NN = (((1,), (0,)), ((), ()))
NT = (((1,), (1,)), ((), ()))
TN = (((0,), (0,)), ((), ()))


def mm(a, b, dims):
    return lax.dot_general(a, b, dims, preferred_element_type=F32)


def one_hot(ids, base, size):
    rows = lax.broadcasted_iota(jnp.int32, (size, ids.shape[1]), 0) + base
    return jnp.where(rows == ids, 1.0, 0.0).astype(BF16)


def layer_kernel(
    reps, tabs, blocks,
    meta, cache_hbm, ids_ref, cot_ref, w_hbm, wo_hbm,
    back_ref, grad_ref,
    cache_v, w_v, wo_v, picked, arrived, emb, normed, hid, proj, att, scores, wts,
    d_att, d_hid, live_cot, gsum, gsend, grecv, gt, tsend, trecv, rowg, rsend, rrecv,
    local_sem, w_s, w_r, wo_s, wo_r, e_s, e_r, g_s, g_r, t_s, t_r, b_s, b_r,
):
    rep = lax.axis_index("replica")
    tab = lax.axis_index("table")
    rows = w_hbm.shape[0]
    cols = cache_hbm.shape[0]
    seq = cot_ref.shape[0]

    def rep_at(i):
        return lax.rem(rep + i, reps)

    def tab_at(i):
        return lax.rem(tab + i, tabs)

    def row_block(r):
        return pl.ds(pl.multiple_of(r * rows, rows), rows)

    own_cache = pltpu.make_async_copy(cache_hbm, cache_v, local_sem.at[0])
    own_w = pltpu.make_async_copy(w_hbm, w_v.at[row_block(rep)], local_sem.at[1])
    own_wo = pltpu.make_async_copy(wo_hbm, wo_v.at[row_block(rep)], local_sem.at[2])
    own_cache.start()
    own_w.start()
    own_wo.start()

    barrier = pltpu.get_barrier_semaphore()

    @pl.loop(1, reps)
    def _(i):
        pl.semaphore_signal(barrier, inc=1, device_id={"replica": rep_at(i)})

    @pl.loop(1, tabs)
    def _(i):
        pl.semaphore_signal(barrier, inc=1, device_id={"table": tab_at(i)})

    pl.semaphore_wait(barrier, reps - 1 + tabs - 1)

    def w_copy(to, source):
        return pltpu.make_async_remote_copy(
            src_ref=w_hbm, dst_ref=w_v.at[row_block(source)],
            send_sem=w_s.at[to], recv_sem=w_r.at[source], device_id={"replica": to})

    def wo_copy(to, source):
        return pltpu.make_async_remote_copy(
            src_ref=wo_hbm, dst_ref=wo_v.at[row_block(source)],
            send_sem=wo_s.at[to], recv_sem=wo_r.at[source], device_id={"replica": to})

    def g_copy(to, source):
        return pltpu.make_async_remote_copy(
            src_ref=gsend.at[row_block(to)], dst_ref=grecv.at[source],
            send_sem=g_s.at[to], recv_sem=g_r.at[source], device_id={"replica": to})

    def e_copy(to, source):
        return pltpu.make_async_remote_copy(
            src_ref=picked.at[to], dst_ref=arrived.at[source],
            send_sem=e_s.at[to], recv_sem=e_r.at[source], device_id={"table": to})

    def t_copy(to, source):
        return pltpu.make_async_remote_copy(
            src_ref=tsend.at[to], dst_ref=trecv.at[source],
            send_sem=t_s.at[to], recv_sem=t_r.at[source], device_id={"table": to})

    def b_copy(to, source):
        return pltpu.make_async_remote_copy(
            src_ref=rsend.at[to], dst_ref=rrecv.at[source],
            send_sem=b_s.at[to], recv_sem=b_r.at[source], device_id={"table": to})

    def start_rep(copy):
        @pl.loop(1, reps)
        def _(i):
            copy(rep_at(i), rep).start()

    def start_tab(copy):
        @pl.loop(1, tabs)
        def _(i):
            copy(tab_at(i), tab).start()

    def recv_tab(copy):
        @pl.loop(1, tabs)
        def _(i):
            copy(tab, tab_at(i)).wait_recv()

    start_rep(w_copy)
    start_rep(wo_copy)

    length = meta[0]
    width = seq // blocks
    at_i = lax.broadcasted_iota(jnp.int32, (seq, seq), 0)
    at_j = lax.broadcasted_iota(jnp.int32, (seq, seq), 1)
    pattern = jnp.zeros((seq, seq), jnp.int32)
    for a in range(blocks):
        for b in range(blocks):
            here = ((at_i >= a * width) & (at_i < (a + 1) * width)
                    & (at_j >= b * width) & (at_j < (b + 1) * width))
            chosen = 1 if a == b else meta[1 + a * blocks + b]
            pattern = jnp.where(here, chosen, pattern)
    allowed = jnp.where((pattern > 0) & (at_j <= at_i) & (at_i < length), 1.0, 0.0)
    live = jnp.where(lax.broadcasted_iota(jnp.int32, (seq, D), 0) < length, 1.0, 0.0)
    cot = cot_ref[...].astype(F32) * live
    live_cot[...] = cot.astype(BF16)

    own_cache.wait()
    ids = ids_ref[...]
    size = min(CHUNK, cache_v.shape[1])
    found = jnp.zeros((cols, ids.shape[1]), F32)
    for m in range(0, cache_v.shape[1], size):
        found = found + mm(
            cache_v[:, m : m + size].astype(BF16), one_hot(ids, m, size), NN)
    for q in range(tabs):
        picked[q] = found[:, q * seq : (q + 1) * seq].astype(BF16)
    start_tab(e_copy)
    arrived[tab] = picked[tab]
    recv_tab(e_copy)
    for q in range(tabs):
        emb[q * cols : (q + 1) * cols, :] = arrived[q].astype(F32)

    e = emb[...]
    centred = e - jnp.mean(e, axis=0, keepdims=True)
    inverse = 1.0 / jnp.sqrt(jnp.mean(centred * centred, axis=0, keepdims=True) + EPS_NORM)
    norm = centred * inverse
    normed[...] = norm.astype(BF16)

    own_w.wait()
    hid[...] = mm(normed[row_block(rep), :], w_v[row_block(rep), :], TN)

    @pl.loop(1, reps)
    def _(i):
        source = rep_at(i)
        w_copy(rep, source).wait_recv()
        hid[...] += mm(normed[row_block(source), :], w_v[row_block(source), :], TN)

    for c in range(0, 4 * D, D):
        h = hid[:, c : c + D]
        proj[:, c : c + D] = (h / (1.0 + jnp.exp(-h))).astype(BF16)

    lane = lax.broadcasted_iota(jnp.int32, (seq, PAIR), 1)
    halves = [lane < HEAD_DIM, lane >= HEAD_DIM]

    def half(x, k):
        return jnp.where(halves[k], x, jnp.zeros_like(x))

    scale = HEAD_DIM ** (-0.5)
    for p in range(HEADS // 2):
        at = p * PAIR
        q2 = proj[:, D + at : D + at + PAIR]
        k2 = proj[:, 2 * D + at : 2 * D + at + PAIR]
        v2 = proj[:, 3 * D + at : 3 * D + at + PAIR]
        total = None
        for k in range(2):
            s = mm(q2, half(k2, k), NT) * scale
            scores[2 * p + k] = s
            w = (s / (1.0 + jnp.exp(-s)) * allowed).astype(BF16)
            wts[2 * p + k] = w
            part = mm(w, half(v2, k), NN)
            total = part if total is None else total + part
        att[:, at : at + PAIR] = total

    a = att[...]
    c_att = a - jnp.mean(a, axis=1, keepdims=True)
    inv_att = 1.0 / jnp.sqrt(jnp.mean(c_att * c_att, axis=1, keepdims=True) + EPS_ATTN)
    y = c_att * inv_att
    gate = proj[:, :D].astype(F32)
    gated = (y * gate).astype(BF16)

    gsum[...] = mm(gated, live_cot[...], TN)
    gsend[...] = gsum[...].astype(BF16)
    start_rep(g_copy)

    own_wo.wait()

    @pl.loop(1, reps)
    def _(i):
        wo_copy(rep, rep_at(i)).wait_recv()

    d_gated = mm(live_cot[...], wo_v[...], NT)

    def silu_grad(v):
        sig = 1.0 / (1.0 + jnp.exp(-v))
        return sig * (1.0 + v * (1.0 - sig))

    def put(at, width_of, value):
        h = hid[:, at : at + width_of]
        d_hid[:, at : at + width_of] = (
            value.astype(BF16).astype(F32) * silu_grad(h)).astype(BF16)

    put(0, D, d_gated * y)
    d_y = d_gated * gate
    d_att[...] = (inv_att * (
        d_y - jnp.mean(d_y, axis=1, keepdims=True)
        - y * jnp.mean(d_y * y, axis=1, keepdims=True))).astype(BF16)

    for p in range(HEADS // 2):
        at = p * PAIR
        q2 = proj[:, D + at : D + at + PAIR]
        k2 = proj[:, 2 * D + at : 2 * D + at + PAIR]
        v2 = proj[:, 3 * D + at : 3 * D + at + PAIR]
        da2 = d_att[:, at : at + PAIR]
        dq = dk = dv = None
        for k in range(2):
            s = scores[2 * p + k]
            dw = mm(da2, half(v2, k), NT).astype(BF16).astype(F32)
            ds = (dw * allowed * silu_grad(s) * scale).astype(BF16)
            dv_k = mm(wts[2 * p + k], half(da2, k), TN)
            dq_k = mm(ds, half(k2, k), NN)
            dk_k = mm(ds, half(q2, k), TN)
            dq = dq_k if dq is None else dq + dq_k
            dk = dk_k if dk is None else dk + dk_k
            dv = dv_k if dv is None else dv + dv_k
        put(D + at, PAIR, dq)
        put(2 * D + at, PAIR, dk)
        put(3 * D + at, PAIR, dv)

    d_norm = mm(w_v[...], d_hid[...], NT)
    e = emb[...]
    centred = e - jnp.mean(e, axis=0, keepdims=True)
    inverse = 1.0 / jnp.sqrt(jnp.mean(centred * centred, axis=0, keepdims=True) + EPS_NORM)
    norm = centred * inverse
    rowg[...] = live_cot[...].astype(F32).T + inverse * (
        d_norm - jnp.mean(d_norm, axis=0, keepdims=True)
        - norm * jnp.mean(d_norm * norm, axis=0, keepdims=True))
    for q in range(tabs):
        rsend[q] = rowg[q * cols : (q + 1) * cols, :].astype(BF16)
    start_tab(b_copy)
    rrecv[tab] = rsend[tab]

    summed = gsum[row_block(rep), :]
    for i in range(1, reps):
        source = rep_at(i)
        g_copy(rep, source).wait_recv()
        summed = summed + grecv[source].astype(F32)
    gt[...] = summed.T
    for q in range(tabs):
        tsend[q] = gt[q * cols : (q + 1) * cols, :].astype(BF16)
    start_tab(t_copy)
    trecv[tab] = tsend[tab]

    recv_tab(b_copy)
    back_ref[...] = rrecv[...]

    recv_tab(t_copy)
    out = trecv[0].astype(F32)
    for q in range(1, tabs):
        out = out + trecv[q].astype(F32)
    grad_ref[...] = out

    for copy in (w_copy, wo_copy, g_copy):
        @pl.loop(1, reps)
        def _(i):
            copy(rep_at(i), rep).wait_send()

    for copy in (e_copy, b_copy, t_copy):
        @pl.loop(1, tabs)
        def _(i):
            copy(tab_at(i), tab).wait_send()


def update_kernel(back_ref, ids_ref, cache_ref, accum_ref, cache_out, accum_out, grads):
    step = pl.program_id(0)
    tabs, _, seq = back_ref.shape
    size = cache_ref.shape[1]

    @pl.when(step == 0)
    def _():
        for q in range(tabs):
            grads[:, q * seq : (q + 1) * seq] = back_ref[q]

    grad = mm(grads[...], one_hot(ids_ref[...], step * size, size), NT)
    accum_next = accum_ref[...] + grad * grad
    accum_out[...] = accum_next
    cache_out[...] = cache_ref[...] - STEP_SIZE * grad / jnp.sqrt(accum_next)


def body(cache, accum, row_ids, lengths, seq_slot, block_mask, cotangent, w_uqkv, w_out, w2_accum):
    reps = lax.axis_size("replica")
    tabs = lax.axis_size("table")
    tab = lax.axis_index("table")
    cols, cached = cache.shape
    rows = w_uqkv.shape[0]
    seq = row_ids.shape[2]
    blocks = block_mask.shape[-1]
    slots = seq_slot.shape[1]

    slot = jnp.arange(slots, dtype=jnp.int32)
    match = seq_slot[0][None, :] == slot[:, None]
    ids = jnp.sum(jnp.where(match[:, :, None], row_ids[0][None], 0), axis=1)
    ids = ids.reshape(1, slots * seq)
    own = seq_slot[0] == tab
    facts = jnp.concatenate(
        [lengths[0][:, None], block_mask[0].reshape(slots, blocks * blocks)], axis=1)
    meta = jnp.sum(jnp.where(own[:, None], facts, 0), axis=0)

    vmem = pl.BlockSpec(memory_space=pltpu.VMEM)
    smem = pl.BlockSpec(memory_space=pltpu.SMEM)
    hbm = pl.BlockSpec(memory_space=pl.ANY)
    dma = pltpu.SemaphoreType.DMA
    V = pltpu.VMEM
    back, grad_t = pl.pallas_call(
        functools.partial(layer_kernel, reps, tabs, blocks),
        out_shape=(
            jax.ShapeDtypeStruct((tabs, cols, seq), BF16),
            jax.ShapeDtypeStruct((cols, rows), F32),
        ),
        in_specs=[smem, hbm, vmem, vmem, hbm, hbm],
        out_specs=(vmem, vmem),
        scratch_shapes=[
            V((cols, cached), F32), V((D, 4 * D), BF16), V((D, D), BF16),
            V((tabs, cols, seq), BF16), V((tabs, cols, seq), BF16), V((D, seq), F32),
            V((D, seq), BF16), V((seq, 4 * D), F32), V((seq, 4 * D), BF16),
            V((seq, D), F32), V((HEADS, seq, seq), F32), V((HEADS, seq, seq), BF16),
            V((seq, D), BF16), V((seq, 4 * D), BF16), V((seq, D), BF16),
            V((D, D), F32), V((D, D), BF16), V((reps, rows, D), BF16),
            V((D, rows), F32), V((tabs, cols, rows), BF16), V((tabs, cols, rows), BF16),
            V((D, seq), F32), V((tabs, cols, seq), BF16), V((tabs, cols, seq), BF16),
            dma((3,)), dma((reps,)), dma((reps,)), dma((reps,)), dma((reps,)),
            dma((tabs,)), dma((tabs,)), dma((reps,)), dma((reps,)),
            dma((tabs,)), dma((tabs,)), dma((tabs,)), dma((tabs,)),
        ],
        compiler_params=pltpu.CompilerParams(
            collective_id=0, has_side_effects=True, vmem_limit_bytes=56 * 1024 * 1024),
        name="layer",
    )(meta, cache, ids, cotangent[0], w_uqkv, w_out)

    size = min(CHUNK, cached)
    block = pl.BlockSpec((cols, size), lambda m: (0, m))
    cache_next, accum_next = pl.pallas_call(
        update_kernel,
        grid=(cached // size,),
        out_shape=(jax.ShapeDtypeStruct(cache.shape, F32),) * 2,
        in_specs=[
            pl.BlockSpec((tabs, cols, seq), lambda m: (0, 0, 0)),
            pl.BlockSpec((1, slots * seq), lambda m: (0, 0)),
            block, block,
        ],
        out_specs=(block, block),
        scratch_shapes=[V((cols, tabs * seq), BF16)],
        compiler_params=pltpu.CompilerParams(vmem_limit_bytes=40 * 1024 * 1024),
        name="update",
    )(back, ids, cache, accum)

    summed = grad_t.T
    w2_step = summed / jnp.sqrt(w2_accum + summed * summed)
    return (cache_next, accum_next, w2_step)


def solution(mesh):
    return jax.shard_map(
        body,
        mesh=mesh,
        in_specs=(
            P("table", "replica"),
            P("table", "replica"),
            P("replica", None, None),
            P("replica", None),
            P("replica", None),
            P("replica", None, None, None),
            P("replica", "table", None),
            P("replica", None),
            P("replica", None),
            P("replica", "table"),
        ),
        out_specs=(P("table", "replica"), P("table", "replica"), P("replica", "table")),
        check_vma=False,
    )
```

time: 181 us -> 105 us (0.58)
  Pallas kernels: 0 us -> 96.8 us
  waiting for transfers between devices: 84.4 us -> 0 us
  local copies, waits for them, and re-layouts: 27.2 us -> 2.66 us
  matrix products: 22.4 us -> 0 us
  other arithmetic: 19.4 us -> 4.92 us
  between operations: 14.2 us -> 0.68 us
  starting transfers between devices: 11.7 us -> 0 us
    pallas_call x0 -> x2, Pallas kernels: none -> 96.8 us  [the longest x1 91 us: body(): pl.pallas_call(functools.partial(layer_kernel, reps, tabs, blocks), out_s...]
    all_gather x2 -> x0, waiting for transfers between devices: 29.8 us -> none  [the longest x1 21.1 us: body(): full_uqkv = lax.all_gather(w_uqkv, 'replica', axis=0, tiled=True)]
    reduce_scatter x1 -> x0, waiting for transfers between devices: 25 us -> none  [body(): lax.psum_scatter(full_grad, 'table', scatter_dimension=1, tiled=True)]
    dot_general x10 -> x0, matrix products: 22.4 us -> none  [the longest x1 5.02 us: body(): lax.dot_general(d_hidden, full_uqkv, (((1,), (1,)), ((), ())), preferred_...]
    all_to_all x2 -> x0, waiting for transfers between devices: 15.8 us -> none  [the longest x1 13 us: body(): lax.all_to_all(sending, 'table', split_axis=0, concat_axis=2, tiled=True)]
    unnamed x5 -> x0, waiting for transfers between devices: 13.8 us -> none
    unnamed x57 -> x10, local copies, waits for them, and re-layouts: 15.3 us -> 2.66 us
    all_to_all x2 -> x0, starting transfers between devices: 11.6 us -> none  [the longest x1 6.34 us: body(): lax.all_to_all(picked, 'table', split_axis=1, concat_axis=0, tiled=True)]
  transfers between devices with their start and end apart: 6 -> 0, of which waited for: 6 -> 0; matrix products, arithmetic and copies ran while one was open for 32% -> 0% of each run, Pallas kernels for 0% -> 0%
where the time goes in v1:
time: 105 us
  Pallas kernels  96.8 us (92%)
  other arithmetic  4.92 us (5%)
  local copies, waits for them, and re-layouts  2.66 us (3%)
    pallas_call x1, Pallas kernels, body(): pl.pallas_call(functools.partial(layer_kernel, reps, tabs, blocks), out_s...  91 us
    pallas_call x1, Pallas kernels, body(): pl.pallas_call(update_kernel, grid=(cached // size,), out_shape=(jax.Shap...  5.76 us
    unnamed x10, local copies, waits for them, and re-layouts  2.66 us

profile of v1, /device:TPU:1, one launch (start us, length us, event | category | flops | bytes accessed | tf_op | source)
XLA Modules:
  0.0 105.0 jit_solution(7441839353362611887)
XLA Ops:
  0.6 0.7 broadcast_compare_fusion
  1.3 1.3 %fusion.2.meta = s32[5]{0:T(128)} fusion(s32[8,4]{0,1:T(4,128)} %bitcast.20, s32[8,1]{0,1:T(1,128)} %bitcast.21, pred[8]{0:T(512)(128)(4,1)S(1)} %broadcast_compare_fusion), kind=kLoop, calls=%fused_computation.6 | loop fusion | flops 115 | bytes 188 | tf_op jit(solution)/shard_map/reduce_sum | solution.py:330
  2.6 0.7 iota_compare_fusion
  3.3 1.4 %select_reduce_fusion = s32[8,128]{1,0:T(8,128)} fusion(s32[8,128]{1,0:T(8,128)} %bitcast.19, pred[8,8]{1,0:T(8,128)(4,1)S(1)} %iota_compare_fusion), kind=kLoop, calls=%fused_computation.4 | loop fusion | flops 15360 | bytes 8256 | tf_op jit(solution)/shard_map/reduce_sum | solution.py:325
  4.6 1.0 copy.15
  5.6 0.0 copy-start
  5.6 0.0 copy-start.1
  5.6 0.0 copy-start.3
  5.7 91.0 %layer.1 = (bf16[8,96,128]{2,1,0:T(8,128)(2,1)}, f32[96,192]{1,0:T(8,128)}) custom-call(s32[5]{0:T(128)} %fusion.2.meta, f32[96,4096]{1,0:T(8,128)} %cache_ref.1, s32[1,1024]{1,0:T(1,128)} %bitcast.16, bf16[128,768]{1,0:T(8,128)(2,1)} %bitcast.18, bf16[192,3072]{1,0:T(8,128)(2,1)} %w_hbm.1, bf16[192,768]{1,0:T(8,128)(2,1)} %wo_hbm.1), custom_call_target="tpu_custom_call" | custom-call | tf_op jit(solution)/shard_map/layer/pallas_call | solution.py:337
  96.7 0.9 bitcast_multiply_fusion
  97.6 0.7 copy.16
  98.3 0.0 copy-done
  98.3 0.0 copy-done.1
  98.3 0.0 copy-done.3
  98.3 0.0 copy-start.2
  98.3 0.9 copy-done.2
  99.3 5.8 %update.1 = (f32[96,4096]{1,0:T(8,128)}, f32[96,4096]{1,0:T(8,128)}) custom-call(bf16[8,96,128]{2,1,0:T(8,128)(2,1)S(1)} %copy-done.2, s32[1,1024]{1,0:T(1,128)S(1)} %bitcast.17, f32[96,4096]{1,0:T(8,128)S(1)} %copy-done, f32[96,4096]{1,0:T(8,128)S(1)} %copy-done.1), custom_call_target="tpu_custom_call" | custom-call | tf_op jit(solution)/shard_map/update/pallas_call | solution.py:365
Async XLA Ops:
  5.6 92.7 %copy-start = (f32[96,4096]{1,0:T(8,128)S(1)}, f32[96,4096]{1,0:T(8,128)}, u32[]{:S(2)}) copy-start(f32[96,4096]{1,0:T(8,128)} %cache_ref.1) | copy-start | bytes 4718596
  5.6 92.7 %copy-start.1 = (f32[96,4096]{1,0:T(8,128)S(1)}, f32[96,4096]{1,0:T(8,128)}, u32[]{:S(2)}) copy-start(f32[96,4096]{1,0:T(8,128)} %accum_ref.1) | copy-start | bytes 4718596
  5.6 92.7 %copy-start.3 = (s32[8,128]{1,0:T(8,128)S(1)}, s32[8,128]{1,0:T(8,128)}, u32[]{:S(2)}) copy-start(s32[8,128]{1,0:T(8,128)} %select_reduce_fusion) | copy-start | bytes 12292
  98.3 0.9 copy-start.2

commit v2 on v1

--- a/solution.py
+++ b/solution.py
@@ -15,6 +15,7 @@
 STEP_SIZE = 0.5
 PAIR = 2 * HEAD_DIM
 CHUNK = 512
+PIECE = D // 2
 
 F32 = jnp.float32
 BF16 = jnp.bfloat16
@@ -35,11 +36,11 @@
 
 def layer_kernel(
     reps, tabs, blocks,
-    meta, cache_hbm, ids_ref, cot_ref, w_hbm, wo_hbm,
-    back_ref, grad_ref,
-    cache_v, w_v, wo_v, picked, arrived, emb, normed, hid, proj, att, scores, wts,
+    slots_ref, lengths_ref, mask_ref, cache_hbm, row_ids_ref, cot_ref, w_hbm, wo_hbm,
+    back_ref, grad_ref, ids_ref,
+    cache_v, w_v, picked, arrived, emb, normed, hid, proj, att, scores, wts,
     d_att, d_hid, live_cot, gsum, gsend, grecv, gt, tsend, trecv, rowg, rsend, rrecv,
-    local_sem, w_s, w_r, wo_s, wo_r, e_s, e_r, g_s, g_r, t_s, t_r, b_s, b_r,
+    local_sem, y_s, x_s, c_s, w_r, e_s, e_r, g_s, g_r, t_s, t_r, b_s, b_r,
 ):
     rep = lax.axis_index("replica")
     tab = lax.axis_index("table")
@@ -57,11 +58,13 @@
         return pl.ds(pl.multiple_of(r * rows, rows), rows)
 
     own_cache = pltpu.make_async_copy(cache_hbm, cache_v, local_sem.at[0])
-    own_w = pltpu.make_async_copy(w_hbm, w_v.at[row_block(rep)], local_sem.at[1])
-    own_wo = pltpu.make_async_copy(wo_hbm, wo_v.at[row_block(rep)], local_sem.at[2])
-    own_cache.start()
+    own_w = pltpu.make_async_copy(
+        w_hbm, w_v.at[row_block(rep), pl.ds(0, 4 * D)], local_sem.at[1])
+    own_wo = pltpu.make_async_copy(
+        wo_hbm, w_v.at[row_block(rep), pl.ds(4 * D, D)], local_sem.at[2])
     own_w.start()
     own_wo.start()
+    own_cache.start()
 
     barrier = pltpu.get_barrier_semaphore()
 
@@ -75,15 +78,65 @@
 
     pl.semaphore_wait(barrier, reps - 1 + tabs - 1)
 
-    def w_copy(to, source):
-        return pltpu.make_async_remote_copy(
-            src_ref=w_hbm, dst_ref=w_v.at[row_block(source)],
-            send_sem=w_s.at[to], recv_sem=w_r.at[source], device_id={"replica": to})
-
-    def wo_copy(to, source):
-        return pltpu.make_async_remote_copy(
-            src_ref=wo_hbm, dst_ref=wo_v.at[row_block(source)],
-            send_sem=wo_s.at[to], recv_sem=wo_r.at[source], device_id={"replica": to})
+    parity = lax.rem(tab, 2)
+    side = lax.rem(rep, 2)
+    mate = rep + 1 - 2 * side
+    beside = tab + 1 - 2 * parity
+    pairs = reps // 2
+    pieces = 5 * D // PIECE
+    steps = pieces // 2
+
+    def piece(source, j):
+        return w_v.at[row_block(source), pl.ds(pl.multiple_of(j * PIECE, PIECE), PIECE)]
+
+    def other(i):
+        return 2 * lax.rem(rep // 2 + i, pairs) + side
+
+    def y_copy(to, source, j):
+        return pltpu.make_async_remote_copy(
+            src_ref=piece(source, j), dst_ref=piece(source, j),
+            send_sem=y_s.at[to, j], recv_sem=w_r.at[source, j], device_id={"replica": to})
+
+    def x_copy(source, j):
+        return pltpu.make_async_remote_copy(
+            src_ref=piece(source, j), dst_ref=piece(source, j),
+            send_sem=x_s.at[source, j], recv_sem=w_r.at[source, j],
+            device_id={"table": beside})
+
+    def c_copy(source, j):
+        return pltpu.make_async_remote_copy(
+            src_ref=piece(source, j), dst_ref=piece(source, j),
+            send_sem=c_s.at[source, j], recv_sem=w_r.at[source, j],
+            device_id={"replica": mate})
+
+    def order(step):
+        return (step + 1) % (steps - 1) if step < steps - 1 else steps - 1
+
+    def relay_direct(step):
+        j = 2 * order(step) + parity
+
+        @pl.loop(1, pairs)
+        def _(i):
+            source = other(i)
+            y_copy(rep, source, j).wait_recv()
+            x_copy(source, j).start()
+            c_copy(source, j).start()
+
+    def relay_beside(step):
+        j = 2 * order(step) + 1 - parity
+
+        @pl.loop(1, pairs)
+        def _(i):
+            source = other(i)
+            x_copy(source, j).wait_recv()
+            c_copy(source, j).start()
+
+    def columns_ready(step):
+        for k in range(2):
+            @pl.loop(0, pairs)
+            def _(i):
+                source = 2 * i + 1 - side
+                c_copy(source, 2 * order(step) + k).wait_recv()
 
     def g_copy(to, source):
         return pltpu.make_async_remote_copy(
@@ -120,10 +173,27 @@
         def _(i):
             copy(tab, tab_at(i)).wait_recv()
 
-    start_rep(w_copy)
-    start_rep(wo_copy)
-
-    length = meta[0]
+    own_w.wait()
+    own_wo.wait()
+    for step in range(steps):
+        j = 2 * order(step) + parity
+
+        @pl.loop(1, pairs)
+        def _(i):
+            y_copy(other(i), rep, j).start()
+
+        c_copy(rep, 2 * order(step)).start()
+        c_copy(rep, 2 * order(step) + 1).start()
+
+    tab_slots = slots_ref.shape[1]
+
+    def own_scalar(value):
+        total = jnp.int32(0)
+        for n in range(tab_slots):
+            total = total + jnp.where(slots_ref[0, n] == tab, value(n), 0)
+        return total
+
+    length = own_scalar(lambda n: lengths_ref[0, n])
     width = seq // blocks
     at_i = lax.broadcasted_iota(jnp.int32, (seq, seq), 0)
     at_j = lax.broadcasted_iota(jnp.int32, (seq, seq), 1)
@@ -132,12 +202,23 @@
         for b in range(blocks):
             here = ((at_i >= a * width) & (at_i < (a + 1) * width)
                     & (at_j >= b * width) & (at_j < (b + 1) * width))
-            chosen = 1 if a == b else meta[1 + a * blocks + b]
+            chosen = 1 if a == b else own_scalar(lambda n: mask_ref[0, n, a, b])
             pattern = jnp.where(here, chosen, pattern)
     allowed = jnp.where((pattern > 0) & (at_j <= at_i) & (at_i < length), 1.0, 0.0)
     live = jnp.where(lax.broadcasted_iota(jnp.int32, (seq, D), 0) < length, 1.0, 0.0)
     cot = cot_ref[...].astype(F32) * live
     live_cot[...] = cot.astype(BF16)
+
+    relay_direct(0)
+
+    row_ids = row_ids_ref[0]
+    at_slot = lax.broadcasted_iota(jnp.int32, row_ids.shape, 0)
+    slot_rows = jnp.zeros_like(row_ids)
+    for n in range(tab_slots):
+        slot_rows = slot_rows + jnp.where(
+            at_slot == slots_ref[0, n], row_ids[n : n + 1, :], 0)
+    for q in range(tab_slots):
+        ids_ref[:, q * seq : (q + 1) * seq] = slot_rows[q : q + 1, :]
 
     own_cache.wait()
     ids = ids_ref[...]
@@ -158,20 +239,24 @@
     centred = e - jnp.mean(e, axis=0, keepdims=True)
     inverse = 1.0 / jnp.sqrt(jnp.mean(centred * centred, axis=0, keepdims=True) + EPS_NORM)
     norm = centred * inverse
-    normed[...] = norm.astype(BF16)
-
-    own_w.wait()
-    hid[...] = mm(normed[row_block(rep), :], w_v[row_block(rep), :], TN)
-
-    @pl.loop(1, reps)
-    def _(i):
-        source = rep_at(i)
-        w_copy(rep, source).wait_recv()
-        hid[...] += mm(normed[row_block(source), :], w_v[row_block(source), :], TN)
-
-    for c in range(0, 4 * D, D):
-        h = hid[:, c : c + D]
-        proj[:, c : c + D] = (h / (1.0 + jnp.exp(-h))).astype(BF16)
+    normed[...] = norm
+
+    rows_normed = normed[...].T.astype(BF16)
+
+    def project(step):
+        columns_ready(step)
+        at = pl.ds(pl.multiple_of(order(step) * 2 * PIECE, 2 * PIECE), 2 * PIECE)
+        h = mm(rows_normed, w_v[:, at], NN)
+        hid[:, at] = h
+        proj[:, at] = (h / (1.0 + jnp.exp(-h))).astype(BF16)
+
+    for step in range(1, steps + 2):
+        if step < steps:
+            relay_direct(step)
+        if step - 1 < steps:
+            relay_beside(step - 1)
+        if 0 <= step - 2 < steps - 1:
+            project(step - 2)
 
     lane = lax.broadcasted_iota(jnp.int32, (seq, PAIR), 1)
     halves = [lane < HEAD_DIM, lane >= HEAD_DIM]
@@ -206,13 +291,8 @@
     gsend[...] = gsum[...].astype(BF16)
     start_rep(g_copy)
 
-    own_wo.wait()
-
-    @pl.loop(1, reps)
-    def _(i):
-        wo_copy(rep, rep_at(i)).wait_recv()
-
-    d_gated = mm(live_cot[...], wo_v[...], NT)
+    columns_ready(steps - 1)
+    d_gated = mm(live_cot[...], w_v[:, 4 * D :], NT)
 
     def silu_grad(v):
         sig = 1.0 / (1.0 + jnp.exp(-v))
@@ -250,7 +330,7 @@
         put(2 * D + at, PAIR, dk)
         put(3 * D + at, PAIR, dv)
 
-    d_norm = mm(w_v[...], d_hid[...], NT)
+    d_norm = mm(w_v[:, : 4 * D], d_hid[...], NT)
     e = emb[...]
     centred = e - jnp.mean(e, axis=0, keepdims=True)
     inverse = 1.0 / jnp.sqrt(jnp.mean(centred * centred, axis=0, keepdims=True) + EPS_NORM)
@@ -283,10 +363,21 @@
         out = out + trecv[q].astype(F32)
     grad_ref[...] = out
 
-    for copy in (w_copy, wo_copy, g_copy):
-        @pl.loop(1, reps)
-        def _(i):
-            copy(rep_at(i), rep).wait_send()
+    for step in range(steps):
+        direct = 2 * order(step) + parity
+        c_copy(rep, direct).wait_send()
+        c_copy(rep, 2 * order(step) + 1 - parity).wait_send()
+
+        @pl.loop(1, pairs)
+        def _(i):
+            y_copy(other(i), rep, direct).wait_send()
+            x_copy(other(i), direct).wait_send()
+            c_copy(other(i), direct).wait_send()
+            c_copy(other(i), 2 * order(step) + 1 - parity).wait_send()
+
+    @pl.loop(1, reps)
+    def _(i):
+        g_copy(rep_at(i), rep).wait_send()
 
     for copy in (e_copy, b_copy, t_copy):
         @pl.loop(1, tabs)
@@ -294,7 +385,9 @@
             copy(tab_at(i), tab).wait_send()
 
 
-def update_kernel(back_ref, ids_ref, cache_ref, accum_ref, cache_out, accum_out, grads):
+def update_kernel(
+    back_ref, ids_ref, grad_ref, w2_ref, cache_ref, accum_ref, cache_out, accum_out, w2_out, grads
+):
     step = pl.program_id(0)
     tabs, _, seq = back_ref.shape
     size = cache_ref.shape[1]
@@ -303,82 +396,78 @@
     def _():
         for q in range(tabs):
             grads[:, q * seq : (q + 1) * seq] = back_ref[q]
+        summed = grad_ref[...].T
+        w2_out[...] = summed * lax.rsqrt(w2_ref[...] + summed * summed)
 
     grad = mm(grads[...], one_hot(ids_ref[...], step * size, size), NT)
     accum_next = accum_ref[...] + grad * grad
     accum_out[...] = accum_next
-    cache_out[...] = cache_ref[...] - STEP_SIZE * grad / jnp.sqrt(accum_next)
+    cache_out[...] = cache_ref[...] - STEP_SIZE * grad * lax.rsqrt(accum_next)
 
 
 def body(cache, accum, row_ids, lengths, seq_slot, block_mask, cotangent, w_uqkv, w_out, w2_accum):
     reps = lax.axis_size("replica")
     tabs = lax.axis_size("table")
-    tab = lax.axis_index("table")
     cols, cached = cache.shape
     rows = w_uqkv.shape[0]
     seq = row_ids.shape[2]
     blocks = block_mask.shape[-1]
     slots = seq_slot.shape[1]
 
-    slot = jnp.arange(slots, dtype=jnp.int32)
-    match = seq_slot[0][None, :] == slot[:, None]
-    ids = jnp.sum(jnp.where(match[:, :, None], row_ids[0][None], 0), axis=1)
-    ids = ids.reshape(1, slots * seq)
-    own = seq_slot[0] == tab
-    facts = jnp.concatenate(
-        [lengths[0][:, None], block_mask[0].reshape(slots, blocks * blocks)], axis=1)
-    meta = jnp.sum(jnp.where(own[:, None], facts, 0), axis=0)
-
     vmem = pl.BlockSpec(memory_space=pltpu.VMEM)
     smem = pl.BlockSpec(memory_space=pltpu.SMEM)
     hbm = pl.BlockSpec(memory_space=pl.ANY)
     dma = pltpu.SemaphoreType.DMA
     V = pltpu.VMEM
-    back, grad_t = pl.pallas_call(
+    pieces = 5 * D // PIECE
+    back, grad_t, ids = pl.pallas_call(
         functools.partial(layer_kernel, reps, tabs, blocks),
         out_shape=(
             jax.ShapeDtypeStruct((tabs, cols, seq), BF16),
             jax.ShapeDtypeStruct((cols, rows), F32),
+            jax.ShapeDtypeStruct((1, slots * seq), jnp.int32),
         ),
-        in_specs=[smem, hbm, vmem, vmem, hbm, hbm],
-        out_specs=(vmem, vmem),
+        in_specs=[smem, smem, smem, hbm, vmem, vmem, hbm, hbm],
+        out_specs=(vmem, vmem, vmem),
         scratch_shapes=[
-            V((cols, cached), F32), V((D, 4 * D), BF16), V((D, D), BF16),
+            V((cols, cached), F32), V((D, 5 * D), BF16),
             V((tabs, cols, seq), BF16), V((tabs, cols, seq), BF16), V((D, seq), F32),
-            V((D, seq), BF16), V((seq, 4 * D), F32), V((seq, 4 * D), BF16),
+            V((D, seq), F32), V((seq, 4 * D), F32), V((seq, 4 * D), BF16),
             V((seq, D), F32), V((HEADS, seq, seq), F32), V((HEADS, seq, seq), BF16),
             V((seq, D), BF16), V((seq, 4 * D), BF16), V((seq, D), BF16),
             V((D, D), F32), V((D, D), BF16), V((reps, rows, D), BF16),
             V((D, rows), F32), V((tabs, cols, rows), BF16), V((tabs, cols, rows), BF16),
             V((D, seq), F32), V((tabs, cols, seq), BF16), V((tabs, cols, seq), BF16),
-            dma((3,)), dma((reps,)), dma((reps,)), dma((reps,)), dma((reps,)),
+            dma((3,)), dma((reps, pieces)), dma((reps, pieces)), dma((reps, pieces)),
+            dma((reps, pieces)),
             dma((tabs,)), dma((tabs,)), dma((reps,)), dma((reps,)),
             dma((tabs,)), dma((tabs,)), dma((tabs,)), dma((tabs,)),
         ],
         compiler_params=pltpu.CompilerParams(
             collective_id=0, has_side_effects=True, vmem_limit_bytes=56 * 1024 * 1024),
         name="layer",
-    )(meta, cache, ids, cotangent[0], w_uqkv, w_out)
+    )(seq_slot, lengths, block_mask, cache, row_ids, cotangent[0], w_uqkv, w_out)
 
     size = min(CHUNK, cached)
     block = pl.BlockSpec((cols, size), lambda m: (0, m))
-    cache_next, accum_next = pl.pallas_call(
+    cache_next, accum_next, w2_step = pl.pallas_call(
         update_kernel,
         grid=(cached // size,),
-        out_shape=(jax.ShapeDtypeStruct(cache.shape, F32),) * 2,
+        out_shape=(jax.ShapeDtypeStruct(cache.shape, F32),) * 2
+        + (jax.ShapeDtypeStruct(w2_accum.shape, F32),),
         in_specs=[
             pl.BlockSpec((tabs, cols, seq), lambda m: (0, 0, 0)),
             pl.BlockSpec((1, slots * seq), lambda m: (0, 0)),
+            pl.BlockSpec((cols, rows), lambda m: (0, 0)),
+            pl.BlockSpec((rows, cols), lambda m: (0, 0)),
             block, block,
         ],
-        out_specs=(block, block),
+        out_specs=(block, block, pl.BlockSpec((rows, cols), lambda m: (0, 0))),
         scratch_shapes=[V((cols, tabs * seq), BF16)],
         compiler_params=pltpu.CompilerParams(vmem_limit_bytes=40 * 1024 * 1024),
         name="update",
-    )(back, ids, cache, accum)
-
-    summed = grad_t.T
-    w2_step = summed / jnp.sqrt(w2_accum + summed * summed)
+    )(back, ids, grad_t, w2_accum, cache, accum)
+
     return (cache_next, accum_next, w2_step)
 
 

time: 105 us -> 66.1 us (0.63)
  Pallas kernels: 96.8 us -> 61.1 us
  other arithmetic: 4.92 us -> 0 us
  local copies, waits for them, and re-layouts: 2.66 us -> 3.85 us
    pallas_call x1, Pallas kernels: 91 us -> 55.5 us  [body(): pl.pallas_call(functools.partial(layer_kernel, reps, tabs, blocks), out_s...]
    reduce_sum x2 -> x0, other arithmetic: 2.68 us -> none  [the longest x1 1.36 us: body(): ids = jnp.sum(jnp.where(match[:, :, None], row_ids[0][None], 0), axis=1)]
    eq x2 -> x0, other arithmetic: 1.32 us -> none  [the longest x1 0.66 us: body(): own = seq_slot[0] == tab]
    unnamed x10 -> x13, local copies, waits for them, and re-layouts: 2.66 us -> 3.85 us
where the time goes in v2:
time: 66.1 us; the launch traced here: 65.6 us
  Pallas kernels  61.1 us (92%)
  local copies, waits for them, and re-layouts  3.85 us (6%)
  between operations  0.67 us (1%)
    pallas_call x1, Pallas kernels, body(): pl.pallas_call(functools.partial(layer_kernel, reps, tabs, blocks), out_s...  55.5 us
    pallas_call x1, Pallas kernels, body(): pl.pallas_call(update_kernel, grid=(cached // size,), out_shape=(jax.Shap...  5.66 us
    unnamed x13, local copies, waits for them, and re-layouts  3.85 us

profile of v2, /device:TPU:1, one launch (start us, length us, event | category | flops | bytes accessed | tf_op | source)
XLA Modules:
  0.0 65.6 jit_solution(15998928523342005615)
XLA Ops:
  0.6 1.4 %copy.13.mask_ref = s32[1,8,2,2]{3,2,1,0:T(2,128)} copy(s32[1,8,2,2]{1,3,2,0:T(2,128)} %param.15) | data formatting | bytes 256 | tf_op args[5]
  2.0 0.0 copy-start
  2.0 0.0 copy-start.1
  2.0 0.0 copy-start.3
  2.0 55.5 %layer.1 = (bf16[8,96,128]{2,1,0:T(8,128)(2,1)}, f32[96,192]{1,0:T(8,128)}, s32[1,1024]{1,0:T(1,128)}) custom-call(s32[1,8]{1,0:T(1,128)} %slots_ref.1, s32[1,8]{1,0:T(1,128)} %lengths_ref.1, s32[1,8,2,2]{3,2,1,0:T(2,128)} %copy.13.mask_ref, f32[96,4096]{1,0:T(8,128)} %cache_ref.1, s32[1,8,128]{2,1,0:T(8,128)} %row_ids_ref.1, bf16[128,768]{1,0:T(8,128)(2,1)} %bitcast.1, ...), custom_call_target="tpu_custom_call" | custom-call | tf_op jit(solution)/shard_map/layer/pallas_call | solution.py:423
  57.5 0.0 copy-done
  57.5 0.0 copy-done.1
  57.5 0.0 copy-done.3
  57.5 0.0 copy-start.2
  57.5 0.9 %copy-done.2 = bf16[8,96,128]{2,1,0:T(8,128)(2,1)S(1)} copy-done((bf16[8,96,128]{2,1,0:T(8,128)(2,1)S(1)}, bf16[8,96,128]{2,1,0:T(8,128)(2,1)}, u32[]{:S(2)}) %copy-start.2) | copy-done | bytes 196632
  58.4 0.0 copy-start.4
  58.4 0.9 %copy-done.4 = f32[96,192]{1,0:T(8,128)S(1)} copy-done((f32[96,192]{1,0:T(8,128)S(1)}, f32[96,192]{1,0:T(8,128)}, u32[]{:S(2)}) %copy-start.4) | copy-done | bytes 73752
  59.3 0.0 copy-start.5
  59.3 0.7 %copy-done.5 = s32[1,1024]{1,0:T(1,128)S(1)} copy-done((s32[1,1024]{1,0:T(1,128)S(1)}, s32[1,1024]{1,0:T(1,128)}, u32[]{:S(2)}) %copy-start.5) | copy-done | bytes 4120
  60.0 5.7 %update.1 = (f32[96,4096]{1,0:T(8,128)}, f32[96,4096]{1,0:T(8,128)}, f32[192,96]{1,0:T(8,128)}) custom-call(bf16[8,96,128]{2,1,0:T(8,128)(2,1)S(1)} %copy-done.2, s32[1,1024]{1,0:T(1,128)S(1)} %copy-done.5, f32[96,192]{1,0:T(8,128)S(1)} %copy-done.4, f32[192,96]{1,0:T(8,128)S(1)} %copy-done.3, f32[96,4096]{1,0:T(8,128)S(1)} %copy-done, f32[96,4096]{1,0:T(8,128)S(1)} %copy-done.1), custom_call_target="tpu_custom_call" | custom-call | tf_op jit(solution)/shard_map/update/pallas_call | solution.py:453
Async XLA Ops:
  2.0 55.5 %copy-start = (f32[96,4096]{1,0:T(8,128)S(1)}, f32[96,4096]{1,0:T(8,128)}, u32[]{:S(2)}) copy-start(f32[96,4096]{1,0:T(8,128)} %cache_ref.1) | copy-start | bytes 4718596
  2.0 55.5 %copy-start.1 = (f32[96,4096]{1,0:T(8,128)S(1)}, f32[96,4096]{1,0:T(8,128)}, u32[]{:S(2)}) copy-start(f32[96,4096]{1,0:T(8,128)} %accum_ref.1) | copy-start | bytes 4718596
  2.0 55.5 %copy-start.3 = (f32[192,96]{1,0:T(8,128)S(1)}, f32[192,96]{1,0:T(8,128)}, u32[]{:S(2)}) copy-start(f32[192,96]{1,0:T(8,128)} %w2_ref.1) | copy-start | bytes 221188
  57.5 0.9 %copy-start.2 = (bf16[8,96,128]{2,1,0:T(8,128)(2,1)S(1)}, bf16[8,96,128]{2,1,0:T(8,128)(2,1)}, u32[]{:S(2)}) copy-start(bf16[8,96,128]{2,1,0:T(8,128)(2,1)} %get-tuple-element.6.back_ref) | copy-start | bytes 589828
  58.4 0.9 %copy-start.4 = (f32[96,192]{1,0:T(8,128)S(1)}, f32[96,192]{1,0:T(8,128)}, u32[]{:S(2)}) copy-start(f32[96,192]{1,0:T(8,128)} %get-tuple-element.8.grad_ref) | copy-start | bytes 221188
  59.3 0.7 %copy-start.5 = (s32[1,1024]{1,0:T(1,128)S(1)}, s32[1,1024]{1,0:T(1,128)}, u32[]{:S(2)}) copy-start(s32[1,1024]{1,0:T(1,128)} %get-tuple-element.7.ids_ref) | copy-start | bytes 12292

commit v3 on v2

--- a/solution.py
+++ b/solution.py
@@ -39,8 +39,8 @@
     slots_ref, lengths_ref, mask_ref, cache_hbm, row_ids_ref, cot_ref, w_hbm, wo_hbm,
     back_ref, grad_ref, ids_ref,
     cache_v, w_v, picked, arrived, emb, normed, hid, proj, att, scores, wts,
-    d_att, d_hid, live_cot, gsum, gsend, grecv, gt, tsend, trecv, rowg, rsend, rrecv,
-    local_sem, y_s, x_s, c_s, w_r, e_s, e_r, g_s, g_r, t_s, t_r, b_s, b_r,
+    d_att, d_hid, live_cot, gsum, gsend, crecv, ysend, yrecv, gt, tsend, trecv, rowg, rsend, rrecv,
+    local_sem, y_s, x_s, c_s, w_r, e_s, e_r, m_s, m_r, g_s, g_r, t_s, t_r, b_s, b_r,
 ):
     rep = lax.axis_index("replica")
     tab = lax.axis_index("table")
@@ -97,6 +97,17 @@
             src_ref=piece(source, j), dst_ref=piece(source, j),
             send_sem=y_s.at[to, j], recv_sem=w_r.at[source, j], device_id={"replica": to})
 
+    def y_send(to, step):
+        j = 2 * order(step) + parity
+        if step < steps - 1:
+            held, at = w_hbm, j
+        else:
+            held, at = wo_hbm, j - 2 * (steps - 1)
+        return pltpu.make_async_remote_copy(
+            src_ref=held.at[:, pl.ds(pl.multiple_of(at * PIECE, PIECE), PIECE)],
+            dst_ref=piece(rep, j),
+            send_sem=y_s.at[to, j], recv_sem=w_r.at[rep, j], device_id={"replica": to})
+
     def x_copy(source, j):
         return pltpu.make_async_remote_copy(
             src_ref=piece(source, j), dst_ref=piece(source, j),
@@ -138,10 +149,16 @@
                 source = 2 * i + 1 - side
                 c_copy(source, 2 * order(step) + k).wait_recv()
 
+    def m_copy(i):
+        return pltpu.make_async_remote_copy(
+            src_ref=gsend.at[row_block(2 * i + 1 - side)], dst_ref=crecv.at[i],
+            send_sem=m_s.at[i], recv_sem=m_r.at[i], device_id={"replica": mate})
+
     def g_copy(to, source):
         return pltpu.make_async_remote_copy(
-            src_ref=gsend.at[row_block(to)], dst_ref=grecv.at[source],
-            send_sem=g_s.at[to], recv_sem=g_r.at[source], device_id={"replica": to})
+            src_ref=ysend.at[to], dst_ref=yrecv.at[source],
+            send_sem=g_s.at[to], recv_sem=g_r.at[source],
+            device_id={"replica": 2 * to + side})
 
     def e_copy(to, source):
         return pltpu.make_async_remote_copy(
@@ -158,11 +175,6 @@
             src_ref=rsend.at[to], dst_ref=rrecv.at[source],
             send_sem=b_s.at[to], recv_sem=b_r.at[source], device_id={"table": to})
 
-    def start_rep(copy):
-        @pl.loop(1, reps)
-        def _(i):
-            copy(rep_at(i), rep).start()
-
     def start_tab(copy):
         @pl.loop(1, tabs)
         def _(i):
@@ -172,16 +184,15 @@
         @pl.loop(1, tabs)
         def _(i):
             copy(tab, tab_at(i)).wait_recv()
+
+    for step in range(steps):
+        @pl.loop(1, pairs)
+        def _(i):
+            y_send(other(i), step).start()
 
     own_w.wait()
     own_wo.wait()
     for step in range(steps):
-        j = 2 * order(step) + parity
-
-        @pl.loop(1, pairs)
-        def _(i):
-            y_copy(other(i), rep, j).start()
-
         c_copy(rep, 2 * order(step)).start()
         c_copy(rep, 2 * order(step) + 1).start()
 
@@ -250,35 +261,40 @@
         hid[:, at] = h
         proj[:, at] = (h / (1.0 + jnp.exp(-h))).astype(BF16)
 
-    for step in range(1, steps + 2):
+    lane = lax.broadcasted_iota(jnp.int32, (seq, PAIR), 1)
+    halves = [lane < HEAD_DIM, lane >= HEAD_DIM]
+
+    def half(x, k):
+        return jnp.where(halves[k], x, jnp.zeros_like(x))
+
+    scale = HEAD_DIM ** (-0.5)
+    def attend(first, last):
+        for p in range(first, last):
+            at = p * PAIR
+            q2 = proj[:, D + at : D + at + PAIR]
+            k2 = proj[:, 2 * D + at : 2 * D + at + PAIR]
+            v2 = proj[:, 3 * D + at : 3 * D + at + PAIR]
+            total = None
+            for k in range(2):
+                s = mm(q2, half(k2, k), NT) * scale
+                scores[2 * p + k] = s
+                w = (s / (1.0 + jnp.exp(-s)) * allowed).astype(BF16)
+                wts[2 * p + k] = w
+                part = mm(w, half(v2, k), NN)
+                total = part if total is None else total + part
+            att[:, at : at + PAIR] = total
+
+    middle = HEADS // 4
+    for step in range(1, steps + 1):
         if step < steps:
             relay_direct(step)
-        if step - 1 < steps:
-            relay_beside(step - 1)
-        if 0 <= step - 2 < steps - 1:
-            project(step - 2)
-
-    lane = lax.broadcasted_iota(jnp.int32, (seq, PAIR), 1)
-    halves = [lane < HEAD_DIM, lane >= HEAD_DIM]
-
-    def half(x, k):
-        return jnp.where(halves[k], x, jnp.zeros_like(x))
-
-    scale = HEAD_DIM ** (-0.5)
-    for p in range(HEADS // 2):
-        at = p * PAIR
-        q2 = proj[:, D + at : D + at + PAIR]
-        k2 = proj[:, 2 * D + at : 2 * D + at + PAIR]
-        v2 = proj[:, 3 * D + at : 3 * D + at + PAIR]
-        total = None
-        for k in range(2):
-            s = mm(q2, half(k2, k), NT) * scale
-            scores[2 * p + k] = s
-            w = (s / (1.0 + jnp.exp(-s)) * allowed).astype(BF16)
-            wts[2 * p + k] = w
-            part = mm(w, half(v2, k), NN)
-            total = part if total is None else total + part
-        att[:, at : at + PAIR] = total
+        relay_beside(step - 1)
+        if step < steps:
+            project(step - 1)
+        if step == steps - 2:
+            attend(0, middle)
+        if step == steps - 1:
+            attend(middle, HEADS // 2)
 
     a = att[...]
     c_att = a - jnp.mean(a, axis=1, keepdims=True)
@@ -289,7 +305,11 @@
 
     gsum[...] = mm(gated, live_cot[...], TN)
     gsend[...] = gsum[...].astype(BF16)
-    start_rep(g_copy)
+
+    @pl.loop(0, pairs)
+    def _(i):
+        m_copy(i).start()
+
 
     columns_ready(steps - 1)
     d_gated = mm(live_cot[...], w_v[:, 4 * D :], NT)
@@ -308,6 +328,16 @@
     d_att[...] = (inv_att * (
         d_y - jnp.mean(d_y, axis=1, keepdims=True)
         - y * jnp.mean(d_y * y, axis=1, keepdims=True))).astype(BF16)
+
+    @pl.loop(0, pairs)
+    def _(i):
+        m_copy(i).wait_recv()
+
+    @pl.loop(1, pairs)
+    def _(i):
+        to = lax.rem(rep // 2 + i, pairs)
+        ysend[to] = (gsum[row_block(2 * to + side), :] + crecv[to].astype(F32)).astype(BF16)
+        g_copy(to, rep // 2).start()
 
     for p in range(HEADS // 2):
         at = p * PAIR
@@ -343,14 +373,16 @@
     start_tab(b_copy)
     rrecv[tab] = rsend[tab]
 
-    summed = gsum[row_block(rep), :]
-    for i in range(1, reps):
-        source = rep_at(i)
-        g_copy(rep, source).wait_recv()
-        summed = summed + grecv[source].astype(F32)
+    summed = gsum[row_block(rep), :] + crecv[rep // 2].astype(F32)
+    for i in range(1, pairs):
+        source = lax.rem(rep // 2 + i, pairs)
+        g_copy(rep // 2, source).wait_recv()
+        summed = summed + yrecv[source].astype(F32)
     gt[...] = summed.T
     for q in range(tabs):
-        tsend[q] = gt[q * cols : (q + 1) * cols, :].astype(BF16)
+        top = q * cols
+        tsend[q, :, :rows] = gt[top : top + cols // 2, :].astype(BF16)
+        tsend[q, :, rows:] = gt[top + cols // 2 : top + cols, :].astype(BF16)
     start_tab(t_copy)
     trecv[tab] = tsend[tab]
 
@@ -361,7 +393,8 @@
     out = trecv[0].astype(F32)
     for q in range(1, tabs):
         out = out + trecv[q].astype(F32)
-    grad_ref[...] = out
+    grad_ref[: cols // 2, :] = out[:, :rows]
+    grad_ref[cols // 2 :, :] = out[:, rows:]
 
     for step in range(steps):
         direct = 2 * order(step) + parity
@@ -370,14 +403,18 @@
 
         @pl.loop(1, pairs)
         def _(i):
-            y_copy(other(i), rep, direct).wait_send()
+            y_send(other(i), step).wait_send()
             x_copy(other(i), direct).wait_send()
             c_copy(other(i), direct).wait_send()
             c_copy(other(i), 2 * order(step) + 1 - parity).wait_send()
 
-    @pl.loop(1, reps)
-    def _(i):
-        g_copy(rep_at(i), rep).wait_send()
+    @pl.loop(0, pairs)
+    def _(i):
+        m_copy(i).wait_send()
+
+    @pl.loop(1, pairs)
+    def _(i):
+        g_copy(lax.rem(rep // 2 + i, pairs), rep // 2).wait_send()
 
     for copy in (e_copy, b_copy, t_copy):
         @pl.loop(1, tabs)
@@ -435,12 +472,15 @@
             V((D, seq), F32), V((seq, 4 * D), F32), V((seq, 4 * D), BF16),
             V((seq, D), F32), V((HEADS, seq, seq), F32), V((HEADS, seq, seq), BF16),
             V((seq, D), BF16), V((seq, 4 * D), BF16), V((seq, D), BF16),
-            V((D, D), F32), V((D, D), BF16), V((reps, rows, D), BF16),
-            V((D, rows), F32), V((tabs, cols, rows), BF16), V((tabs, cols, rows), BF16),
+            V((D, D), F32), V((D, D), BF16), V((reps // 2, rows, D), BF16),
+            V((reps // 2, rows, D), BF16), V((reps // 2, rows, D), BF16),
+            V((D, rows), F32), V((tabs, cols // 2, 2 * rows), BF16),
+            V((tabs, cols // 2, 2 * rows), BF16),
             V((D, seq), F32), V((tabs, cols, seq), BF16), V((tabs, cols, seq), BF16),
             dma((3,)), dma((reps, pieces)), dma((reps, pieces)), dma((reps, pieces)),
             dma((reps, pieces)),
-            dma((tabs,)), dma((tabs,)), dma((reps,)), dma((reps,)),
+            dma((tabs,)), dma((tabs,)), dma((reps // 2,)), dma((reps // 2,)),
+            dma((reps // 2,)), dma((reps // 2,)),
             dma((tabs,)), dma((tabs,)), dma((tabs,)), dma((tabs,)),
         ],
         compiler_params=pltpu.CompilerParams(
@@ -464,7 +504,7 @@
         ],
         out_specs=(block, block, pl.BlockSpec((rows, cols), lambda m: (0, 0))),
         scratch_shapes=[V((cols, tabs * seq), BF16)],
-        compiler_params=pltpu.CompilerParams(vmem_limit_bytes=40 * 1024 * 1024),
+        compiler_params=pltpu.CompilerParams(vmem_limit_bytes=62 * 1024 * 1024),
         name="update",
     )(back, ids, grad_t, w2_accum, cache, accum)
 

time: 66.1 us -> 65.9 us (level)
  the two profiles are of different devices: /device:TPU:1 before, /device:TPU:0 now
where the time goes in v3:
time: 65.9 us; the launch traced here: 65.6 us
  Pallas kernels  63.6 us (97%)
  local copies, waits for them, and re-layouts  1.36 us (2%)
    pallas_call x1, Pallas kernels, body(): pl.pallas_call(functools.partial(layer_kernel, reps, tabs, blocks), out_s...  55.4 us
    pallas_call x1, Pallas kernels, body(): pl.pallas_call(update_kernel, grid=(cached // size,), out_shape=(jax.Shap...  8.22 us
    unnamed x1, local copies, waits for them, and re-layouts  1.36 us

profile of v3, /device:TPU:0, one launch (start us, length us, event | category | flops | bytes accessed | tf_op | source)
XLA Modules:
  0.0 65.6 jit_solution(2009557988361824210)
XLA Ops:
  0.6 1.4 %copy.13.mask_ref = s32[1,8,2,2]{3,2,1,0:T(2,128)} copy(s32[1,8,2,2]{1,3,2,0:T(2,128)} %param.15) | data formatting | bytes 256 | tf_op args[5]
  2.0 55.4 %layer.1 = (bf16[8,96,128]{2,1,0:T(8,128)(2,1)}, f32[96,192]{1,0:T(8,128)}, s32[1,1024]{1,0:T(1,128)}) custom-call(s32[1,8]{1,0:T(1,128)} %slots_ref.1, s32[1,8]{1,0:T(1,128)} %lengths_ref.1, s32[1,8,2,2]{3,2,1,0:T(2,128)} %copy.13.mask_ref, f32[96,4096]{1,0:T(8,128)} %cache_ref.1, s32[1,8,128]{2,1,0:T(8,128)} %row_ids_ref.1, bf16[128,768]{1,0:T(8,128)(2,1)} %bitcast.1, ...), custom_call_target="tpu_custom_call" | custom-call | tf_op jit(solution)/shard_map/layer/pallas_call | solution.py:460
  57.4 8.2 %update.1 = (f32[96,4096]{1,0:T(8,128)}, f32[96,4096]{1,0:T(8,128)}, f32[192,96]{1,0:T(8,128)}) custom-call(bf16[8,96,128]{2,1,0:T(8,128)(2,1)} %get-tuple-element.6.back_ref, s32[1,1024]{1,0:T(1,128)} %get-tuple-element.7.ids_ref, f32[96,192]{1,0:T(8,128)} %get-tuple-element.8.grad_ref, f32[192,96]{1,0:T(8,128)} %w2_ref.1, f32[96,4096]{1,0:T(8,128)} %cache_ref.1, ...), custom_call_target="tpu_custom_call" | custom-call | tf_op jit(solution)/shard_map/update/pallas_call | solution.py:493
